TPU v7x, 32 devices: a whole 2x2x4 slice. The times are simulated.
32 devices in a mesh: groups: 2 (over y), pulse: 4 (over z), range: 2 (over x), sub: 2 (over core).
Axes of the slice: x: 2, y: 2, z: 4, core: 2. Of those that a mesh axis runs over, the one named last changes fastest.
Arguments:
- raw_echo: bfloat16 [2, 128, 16384], P(None, ('groups', 'pulse', 'sub'), 'range'), parts along dimension 1, may hold values from -6 to 6
- range_taps: bfloat16 [32, 512, 128], P('pulse'), may hold values from -0.25 to 0.25
- azim_taps: bfloat16 [128, 2048], P(('groups', 'pulse', 'sub')), parts along dimension 0, may hold values from -1 to 1
- tile_col: int32 [128, 1], P(('groups', 'pulse', 'sub')), parts along dimension 0, may hold values from 0 to 1; in each aligned block of 4 rows (0 to 3, 4 to 7, ...) at most 2 rows name the same one
Outputs:
- image: float32 [2, 8192, 4096], P(None, ('groups', 'pulse', 'range', 'sub')), parts along dimension 1
There are 2 independent parts, one for each index of `groups`. A program takes and returns all parts, laid end to end along the dimension named above; an argument that names none is the same for every part. Nothing has to cross between parts.
Inputs may be any that keep to these rules, and one draw needn't show every extreme that they name: `tile_col`: in each aligned block of 4 pulses no tile column is named by more than 2 pulses.
All inputs are finite; a program needn't handle non-finite values.
Results may differ from a plain program's by a relative error of at most 0.008.
Values may be sent and summed in bfloat16 or wider, within the bound.
No kernel may reach another device: no remote copies, remote signals or barrier semaphores. Data moves between devices by JAX's collectives and lax.ppermute only.
A program may use at most 64 MiB of HBM per device.

v0:
```python
import math
import jax
import jax.numpy as jnp
from jax import lax
from jax.sharding import PartitionSpec as P

CAP = 2


def swapped(block, axis, bit):
    count = lax.axis_size(axis)
    route = []
    for low in range(count):
        high = low | 1 << bit
        if high != low and high < count:
            route += [(low, high), (high, low)]
    return lax.ppermute(block, axis, route)


def as_sent(value):
    return jax.tree.map(lambda a: a.astype(jnp.bfloat16) if a.dtype == jnp.float32 else a, value)


def tables(points, direction):
    indices = jnp.arange(points, dtype=jnp.int32)
    phases = indices[:, None] * indices[None, :] % points
    angles = phases.astype(jnp.float32) * (2.0 * math.pi / points)
    return (jnp.cos(angles), direction * jnp.sin(angles))


def spectral(real_part, imag_part, direction):
    length = real_part.shape[-1]
    outer_len = 1 << (length.bit_length() - 1) // 2
    inner_len = length // outer_len
    leading = real_part.shape[:-1]
    real_part = real_part.reshape(leading + (outer_len, inner_len))
    imag_part = imag_part.reshape(leading + (outer_len, inner_len))
    highest = lax.Precision.HIGHEST
    cos_outer, sin_outer = tables(outer_len, direction)
    mixed_real = jnp.einsum(
        "...nm,nk->...km", real_part, cos_outer, precision=highest
    ) - jnp.einsum("...nm,nk->...km", imag_part, sin_outer, precision=highest)
    mixed_imag = jnp.einsum(
        "...nm,nk->...km", real_part, sin_outer, precision=highest
    ) + jnp.einsum("...nm,nk->...km", imag_part, cos_outer, precision=highest)
    outer_index = jnp.arange(outer_len, dtype=jnp.int32)[:, None]
    inner_index = jnp.arange(inner_len, dtype=jnp.int32)[None, :]
    twists = (outer_index * inner_index % length).astype(jnp.float32) * (2.0 * math.pi / length)
    twist_cos = jnp.cos(twists)
    twist_sin = direction * jnp.sin(twists)
    turned_real = mixed_real * twist_cos - mixed_imag * twist_sin
    turned_imag = mixed_real * twist_sin + mixed_imag * twist_cos
    cos_inner, sin_inner = tables(inner_len, direction)
    final_real = jnp.einsum(
        "...km,mj->...jk", turned_real, cos_inner, precision=highest
    ) - jnp.einsum("...km,mj->...jk", turned_imag, sin_inner, precision=highest)
    final_imag = jnp.einsum(
        "...km,mj->...jk", turned_real, sin_inner, precision=highest
    ) + jnp.einsum("...km,mj->...jk", turned_imag, cos_inner, precision=highest)
    norm_scale = 1.0 / math.sqrt(length)
    return (
        (final_real * norm_scale).reshape(leading + (length,)),
        (final_imag * norm_scale).reshape(leading + (length,)),
    )


def body(raw_echo, range_taps, azim_taps, tile_col):
    n_range = lax.axis_size("range")
    n_pulse = lax.axis_size("pulse")
    my_range = lax.axis_index("range")
    my_sub = lax.axis_index("sub")
    shard_pulses = raw_echo.shape[1]
    shard_samples = raw_echo.shape[2]
    per_device = shard_pulses // n_range
    grouped = raw_echo.reshape(2, n_range, per_device, shard_samples)
    pieces = lax.all_to_all(grouped, "range", split_axis=1, concat_axis=3, tiled=True)
    real_out, imag_out = spectral(
        pieces[0].astype(jnp.float32), pieces[1].astype(jnp.float32), -1.0
    )
    spectrum = jnp.stack([real_out, imag_out]).astype(jnp.bfloat16)
    spectrum = spectrum.reshape(2, per_device, shard_samples * n_range)
    band_bins = spectrum.shape[2] // n_pulse
    first_pulse = my_range * per_device
    cols_here = lax.dynamic_slice_in_dim(tile_col[:, 0], first_pulse, per_device)
    taps_here = lax.dynamic_slice_in_dim(azim_taps, first_pulse, per_device, 0)
    position = jnp.arange(per_device, dtype=jnp.int32)
    earlier = position[None, :] < position[:, None]
    same_tile = cols_here[:, None] == cols_here[None, :]
    slot_rank = jnp.sum(jnp.where(earlier & same_tile, 1, 0), axis=1)
    tile_ids = jnp.arange(n_range, dtype=jnp.int32)
    slot_ids = jnp.arange(CAP, dtype=jnp.int32)
    placing = (
        (cols_here[None, None, :] == tile_ids[:, None, None])
        & (slot_rank[None, None, :] == slot_ids[None, :, None])
    ).astype(jnp.bfloat16)
    banded = spectrum.reshape(2, per_device, n_pulse, band_bins)
    send_lines = jnp.einsum(
        "tcq,xqpb->ptcxb", placing, banded, preferred_element_type=jnp.float32
    ).astype(jnp.bfloat16)
    send_taps = jnp.einsum(
        "tcq,qw->tcw", placing, taps_here, preferred_element_type=jnp.float32
    ).astype(jnp.bfloat16)
    tile_width = send_taps.shape[2]
    send_taps = jnp.broadcast_to(send_taps[None], (n_pulse, n_range, CAP, tile_width))
    block_count, block_bins, block_rows = range_taps.shape
    flat_lines = send_lines.reshape(n_pulse * n_range, CAP, 2, band_bins)
    flat_taps = send_taps.reshape(n_pulse * n_range, CAP, tile_width)
    line_block = lax.all_to_all(
        flat_lines, ("pulse", "range"), split_axis=0, concat_axis=0, tiled=True
    )
    tap_block = lax.all_to_all(
        flat_taps, ("pulse", "range"), split_axis=0, concat_axis=0, tiled=True
    )
    blocked = line_block.reshape(line_block.shape[:3] + (block_count, block_bins))
    resampled = jnp.einsum(
        "skxbr,brj->skxbj", blocked, range_taps, preferred_element_type=jnp.float32
    )
    ky_rows = resampled.reshape(line_block.shape[:3] + (block_count * block_rows,)).astype(
        jnp.bfloat16
    )
    band_rows = ky_rows.shape[3]
    slot_total = ky_rows.shape[0] * ky_rows.shape[1]
    slot_lines = ky_rows.reshape(slot_total, 2, band_rows)
    slot_taps = tap_block.reshape(slot_total, tile_width)
    half_width = tile_width // 2
    other_lines, other_taps = swapped((slot_lines, slot_taps), "sub", 0)
    column_start = my_sub * half_width
    my_taps = lax.dynamic_slice_in_dim(slot_taps, column_start, half_width, 1)
    their_taps = lax.dynamic_slice_in_dim(other_taps, column_start, half_width, 1)
    own_part = jnp.einsum("mi,mxj->xij", my_taps, slot_lines, preferred_element_type=jnp.float32)
    far_part = jnp.einsum(
        "mi,mxj->xij", their_taps, other_lines, preferred_element_type=jnp.float32
    )
    own_round = lax.optimization_barrier(own_part.astype(jnp.bfloat16))
    far_round = lax.optimization_barrier(far_part.astype(jnp.bfloat16))
    kspace = own_round.astype(jnp.float32) + far_round.astype(jnp.float32)
    pieces_each = half_width // n_pulse
    shaped = kspace.reshape(2, n_pulse, pieces_each, band_rows)
    pieces = lax.all_to_all(
        shaped.astype(jnp.bfloat16), "pulse", split_axis=1, concat_axis=3, tiled=True
    ).astype(shaped.dtype)
    real_out, imag_out = spectral(pieces[0], pieces[1], 1.0)
    columns_done = jnp.stack([real_out, imag_out])
    columns_done = columns_done.reshape(2, pieces_each, band_rows * n_pulse)
    moved = lax.all_to_all(
        lax.all_to_all(as_sent(columns_done), "pulse", split_axis=2, concat_axis=1, tiled=True),
        ("range", "sub"),
        split_axis=2,
        concat_axis=1,
        tiled=True,
    ).astype(columns_done.dtype)
    flipped = jnp.swapaxes(moved, 1, 2)
    real_out, imag_out = spectral(flipped[0], flipped[1], 1.0)
    return jnp.stack([real_out, imag_out])


def solution(mesh):
    placed = (
        P(None, ("groups", "pulse", "sub"), "range"),
        P("pulse", None, None),
        P(("groups", "pulse", "sub"), None),
        P(("groups", "pulse", "sub"), None),
    )
    return jax.shard_map(
        body,
        mesh=mesh,
        in_specs=placed,
        out_specs=P(None, ("groups", "pulse", "range", "sub"), None),
        check_vma=False,
    )
```

profile of v0, /device:TPU:0, one launch (start us, length us, event | category | flops | bytes accessed | tf_op | source)
XLA Modules:
  0.0 452.2 jit_solution(6309015719633737124)
XLA Ops:
  0.0 1.3 copy.126
  1.3 0.9 copy.127
  2.2 4.2 all-to-all-start
  6.5 0.3 fusion.119
  6.7 0.3 sine_multiply_fusion
  7.0 0.7 fusion.182
  7.7 0.2 select_reduce_fusion
  8.1 0.9 convolution_convert_fusion.1
  9.0 3.3 all-to-all-done
  12.3 0.7 broadcast_in_dim.10
  13.0 5.1 %all-to-all-start.2 = ((bf16[8,2,2048]{2,1,0:T(2,128)(2,1)}), bf16[8,2,2048]{2,1,0:T(2,128)(2,1)S(1)}, u32[]{:S(2)}, u32[]{:S(2)}) async-start(bf16[8,2,2048]{2,1,0:T(2,128)(2,1)} %bitcast.30), calls=%async_computation.2 | async-start | bytes 131072 | tf_op jit(solution)/shard_map/all_to_all | solution.py:111
  18.5 0.5 fusion.67
  19.0 0.5 fusion.73
  19.7 0.5 fusion.44
  20.2 0.5 fusion.45
  20.7 0.7 fusion.57
  21.4 0.7 fusion.59
  22.1 0.7 fusion.48
  22.9 0.7 fusion.49
  23.7 0.5 convolution_convert_fusion
  24.2 1.0 copy.134
  25.2 6.3 %all-to-all-start.1 = ((bf16[8,2,2,4096]{3,2,1,0:T(2,128)(2,1)}), bf16[8,2,2,4096]{3,2,1,0:T(2,128)(2,1)S(1)}, u32[]{:S(2)}, u32[]{:S(2)}) async-start(bf16[8,2,2,4096]{3,2,1,0:T(2,128)(2,1)} %copy.134), calls=%async_computation.1 | async-start | bytes 524288 | tf_op jit(solution)/shard_map/all_to_all | solution.py:108
  31.6 8.1 %all-to-all-done.1 = bf16[8,2,2,4096]{3,2,1,0:T(2,128)(2,1)S(1)} async-done(((bf16[8,2,2,4096]{3,2,1,0:T(2,128)(2,1)}), bf16[8,2,2,4096]{3,2,1,0:T(2,128)(2,1)S(1)}, u32[]{:S(2)}, u32[]{:S(2)}) %all-to-all-start.1) | async-done | bytes 262176 | tf_op jit(solution)/shard_map/all_to_all | solution.py:108
  39.9 0.3 fusion.50
  40.4 1.3 convert_bitcast_fusion.1
  41.7 1.3 convert_bitcast_fusion
  42.9 2.2 add_convert_fusion
  45.2 2.3 copy.221
  47.5 5.4 %all-to-all-start.3 = ((bf16[2,4,256,1024]{2,3,0,1:T(8,128)(2,1)}), bf16[2,4,256,1024]{2,3,0,1:T(8,128)(2,1)}, u32[]{:S(2)}, u32[]{:S(2)}) async-start(bf16[2,4,256,1024]{2,3,0,1:T(8,128)(2,1)} %bitcast.216), calls=%async_computation.3 | async-start | bytes 8388608 | tf_op jit(solution)/shard_map/all_to_all | solution.py:139
  53.0 93.5 %all-to-all-done.3 = bf16[2,4,256,1024]{2,3,0,1:T(8,128)(2,1)} async-done(((bf16[2,4,256,1024]{2,3,0,1:T(8,128)(2,1)}), bf16[2,4,256,1024]{2,3,0,1:T(8,128)(2,1)}, u32[]{:S(2)}, u32[]{:S(2)}) %all-to-all-start.3) | async-done | bytes 4194336 | tf_op jit(solution)/shard_map/all_to_all | solution.py:139
  146.5 2.5 copy.222
  148.9 0.3 fusion.261
  149.2 2.8 fusion.38
  152.0 2.8 fusion.40
  154.9 2.9 convolution_add_fusion.1
  157.7 4.7 %fusion.1 = (f32[256,64,64]{0,1,2:T(8,128)S(1)}, f32[256,64,64]{0,1,2:T(8,128)S(1)}) fusion(f32[64,256,64]{1,0,2:T(8,128)S(1)} %convolution_add_fusion.1, f32[64,64]{0,1:T(8,128)S(1)} %get-tuple-element.17, f32[64,64]{0,1:T(8,128)S(1)} %get-tuple-element.18, f32[64,256,64]{1,0,2:T(8,128)S(1)} %fusion.40, bf16[256,64,64]{0,2,1:T(8,128)(2,1)S(1)} %bitcast.210), kind=kOutput, calls=%fused_computation.8 | convolution fusion | flops 812703744 | bytes 18907136 | tf_op jit(solution)/shard_map/...nm,nk->...km/dot_general | solution.py:42
  162.4 6.3 %fusion.12 = f32[64,256,64]{1,0,2:T(8,128)S(1)} fusion(f32[256,64,64]{0,1,2:T(8,128)S(1)} %get-tuple-element.8), kind=kOutput, calls=%fused_computation.30 | convolution fusion | flops 805363712 | bytes 8388608 | tf_op jit(solution)/shard_map/...km,mj->...jk/dot_general | solution.py:59
  168.7 6.5 %fusion.14 = f32[64,256,64]{1,0,2:T(8,128)S(1)} fusion(f32[256,64,64]{0,1,2:T(8,128)S(1)} %get-tuple-element.8), kind=kOutput, calls=%fused_computation.32 | convolution fusion | flops 805363712 | bytes 8388608 | tf_op jit(solution)/shard_map/...km,mj->...jk/dot_general | solution.py:56
  175.2 6.0 %fusion.25 = bf16[1,256,64,64]{1,2,3,0:T(8,128)(2,1)S(1)} fusion(f32[64,256,64]{1,0,2:T(8,128)S(1)} %fusion.12, f32[256,64,64]{0,1,2:T(8,128)S(1)} %get-tuple-element.7), kind=kOutput, calls=%fused_computation.44 | convolution fusion | flops 808509440 | bytes 10485760 | tf_op jit(solution)/shard_map/...km,mj->...jk/dot_general | solution.py:57
  181.2 1.2 copy.149
  182.4 5.9 %fusion.24 = bf16[1,256,64,64]{1,2,3,0:T(8,128)(2,1)S(1)} fusion(f32[64,256,64]{1,0,2:T(8,128)S(1)} %fusion.14, f32[256,64,64]{0,1,2:T(8,128)S(1)} %get-tuple-element.7), kind=kOutput, calls=%fused_computation.43 | convolution fusion | flops 808509440 | bytes 10485760 | tf_op jit(solution)/shard_map/...km,mj->...jk/dot_general | solution.py:54
  188.3 1.2 copy.146
  189.5 0.4 maximum_bitcast_fusion
  189.9 25.5 %copy.150 = bf16[2,256,4096]{1,0,2:T(2,128)(2,1)S(1)} copy(bf16[2,256,4096]{1,2,0:T(8,128)(2,1)S(1)} %maximum_bitcast_fusion) | data formatting | bytes 8388608 | tf_op jit(solution)/shard_map/convert_element_type | solution.py:21
  215.4 95.8 %all_to_all.76 = bf16[2,256,4096]{1,0,2:T(2,128)(2,1)S(1)} all-to-all(bf16[2,256,4096]{1,0,2:T(2,128)(2,1)S(1)} %copy.150), channel_id=1, replica_groups=mesh['groups'=2,'pulse'=4,'range'=2,'sub'=2] {'pulse'}, dimensions={2} | all-to-all | bytes 8388608 | tf_op jit(solution)/shard_map/all_to_all | solution.py:146
  311.2 2.6 copy.151
  313.7 6.3 %copy.152 = bf16[2,4,256,1024]{3,2,1,0:T(8,128)(2,1)} copy(bf16[2,4,256,1024]{2,3,1,0:T(8,128)(2,1)} %bitcast.219) | data formatting | bytes 8388608 | tf_op jit(solution)/shard_map/all_to_all | solution.py:146
  320.0 11.3 %copy.153 = bf16[2,1024,1024]{1,0,2:T(2,128)(2,1)} copy(bf16[2,1024,1024]{2,1,0:T(8,128)(2,1)} %bitcast.220) | data formatting | bytes 8388608 | tf_op jit(solution)/shard_map/all_to_all | solution.py:146
  331.2 51.9 %all_to_all.77 = bf16[2,1024,1024]{1,0,2:T(2,128)(2,1)S(1)} all-to-all(bf16[2,1024,1024]{1,0,2:T(2,128)(2,1)} %copy.153), channel_id=1, replica_groups=mesh['groups'=2,'pulse'=4,'range'=2,'sub'=2] {'range','sub'}, dimensions={2} | all-to-all | bytes 8388608 | tf_op jit(solution)/shard_map/all_to_all | solution.py:145
  383.1 3.3 copy.154
  386.5 6.4 %copy.155 = bf16[2,4,1024,256]{3,2,1,0:T(8,128)(2,1)} copy(bf16[2,4,1024,256]{2,3,1,0:T(8,128)(2,1)} %bitcast.221) | data formatting | bytes 8388608 | tf_op jit(solution)/shard_map/all_to_all | solution.py:145
  392.8 2.5 fusion.260
  395.3 2.8 fusion.32
  398.1 2.8 fusion.34
  401.0 2.9 convolution_add_fusion
  403.9 4.7 %subtract_bitcast_fusion = (f32[256,64,64]{0,1,2:T(8,128)S(1)}, f32[256,64,64]{0,1,2:T(8,128)S(1)}) fusion(f32[64,256,64]{1,0,2:T(8,128)S(1)} %convolution_add_fusion, f32[64,64]{0,1:T(8,128)S(1)} %get-tuple-element.17, f32[64,64]{0,1:T(8,128)S(1)} %get-tuple-element.18, f32[64,256,64]{1,0,2:T(8,128)S(1)} %fusion.34, bf16[256,64,64]{0,2,1:T(8,128)(2,1)S(1)} %bitcast.208), kind=kOutput, calls=%fused_computation.17 | convolution fusion | flops 812703744 | bytes 18907136 | tf_op jit(solution)/shard_map/...nm,nk->...km/dot_general | solution.py:42
  408.6 6.0 %fusion.4 = f32[64,256,64]{1,0,2:T(8,128)S(1)} fusion(f32[256,64,64]{0,1,2:T(8,128)S(1)} %get-tuple-element.6), kind=kOutput, calls=%fused_computation.22 | convolution fusion | flops 805363712 | bytes 8388608 | tf_op jit(solution)/shard_map/...km,mj->...jk/dot_general | solution.py:59
  414.6 6.7 %fusion.6 = f32[64,256,64]{1,0,2:T(8,128)S(1)} fusion(f32[256,64,64]{0,1,2:T(8,128)S(1)} %get-tuple-element.6), kind=kOutput, calls=%fused_computation.24 | convolution fusion | flops 805363712 | bytes 8388608 | tf_op jit(solution)/shard_map/...km,mj->...jk/dot_general | solution.py:56
  421.3 6.4 %multiply_bitcast_fusion.1 = f32[256,64,64]{0,1,2:T(8,128)S(1)} fusion(f32[64,256,64]{1,0,2:T(8,128)S(1)} %fusion.6, f32[256,64,64]{0,1,2:T(8,128)S(1)} %get-tuple-element.5), kind=kOutput, calls=%fused_computation.15 | convolution fusion | flops 807460864 | bytes 12582912 | tf_op jit(solution)/shard_map/...km,mj->...jk/dot_general | solution.py:54
  427.7 6.7 %multiply_bitcast_fusion = f32[256,64,64]{0,1,2:T(8,128)S(1)} fusion(f32[64,256,64]{1,0,2:T(8,128)S(1)} %fusion.4, f32[256,64,64]{0,1,2:T(8,128)S(1)} %get-tuple-element.5), kind=kOutput, calls=%fused_computation.14 | convolution fusion | flops 807460864 | bytes 12582912 | tf_op jit(solution)/shard_map/...km,mj->...jk/dot_general | solution.py:57
  434.4 2.4 copy.165
  436.9 2.4 copy.162
  439.3 3.8 pad_maximum_fusion
  443.1 9.0 %copy.166 = f32[2,256,4096]{2,1,0:T(8,128)} copy(f32[2,256,4096]{1,2,0:T(8,128)} %pad_maximum_fusion) | data formatting | bytes 16777216 | tf_op jit(solution)/shard_map/stack | solution.py:154
  (26 shorter events, 1.6 us)
Async XLA Ops:
  0.0 39.9 %copy-start = (bf16[8,512,128]{2,1,0:T(8,128)(2,1)S(1)}, bf16[8,512,128]{2,1,0:T(8,128)(2,1)}, u32[]{:S(2)}) copy-start(bf16[8,512,128]{2,1,0:T(8,128)(2,1)} %param.5) | copy-start | bytes 3145732
  2.2 10.1 %all-to-all-start = ((bf16[2,2,4,8192]{3,2,0,1:T(4,128)(2,1)}), bf16[2,2,4,8192]{3,2,0,1:T(4,128)(2,1)S(1)}, u32[]{:S(2)}, u32[]{:S(2)}) async-start(bf16[2,2,4,8192]{3,2,0,1:T(4,128)(2,1)} %copy.127), calls=%async_computation | async-start | bytes 524288 | tf_op jit(solution)/shard_map/all_to_all | solution.py:76
  13.0 12.2 %all-to-all-start.2 = ((bf16[8,2,2048]{2,1,0:T(2,128)(2,1)}), bf16[8,2,2048]{2,1,0:T(2,128)(2,1)S(1)}, u32[]{:S(2)}, u32[]{:S(2)}) async-start(bf16[8,2,2048]{2,1,0:T(2,128)(2,1)} %bitcast.30), calls=%async_computation.2 | async-start | bytes 131072 | tf_op jit(solution)/shard_map/all_to_all | solution.py:111
  25.2 14.5 %all-to-all-start.1 = ((bf16[8,2,2,4096]{3,2,1,0:T(2,128)(2,1)}), bf16[8,2,2,4096]{3,2,1,0:T(2,128)(2,1)S(1)}, u32[]{:S(2)}, u32[]{:S(2)}) async-start(bf16[8,2,2,4096]{3,2,1,0:T(2,128)(2,1)} %copy.134), calls=%async_computation.1 | async-start | bytes 524288 | tf_op jit(solution)/shard_map/all_to_all | solution.py:108
  31.5 10.1 %collective-permute-start.1 = (bf16[16,2048]{1,0:T(8,128)(2,1)S(1)}, bf16[16,2048]{1,0:T(8,128)(2,1)S(1)}, u32[]{:S(2)}, u32[]{:S(2)}) collective-permute-start(bf16[16,2048]{1,0:T(8,128)(2,1)S(1)} %reshape.306), channel_id=1, source_target_pairs={{0,1},{1,0},{2,3},{3,2},{4,5},{5,4},{6,7},{7,6},{8,9},{9,8},{10,11... | collective-permute-start | bytes 196616 | tf_op jit(solution)/shard_map/ppermute | solution.py:17
  40.3 1.4 collective-permute-start
  47.5 99.0 %all-to-all-start.3 = ((bf16[2,4,256,1024]{2,3,0,1:T(8,128)(2,1)}), bf16[2,4,256,1024]{2,3,0,1:T(8,128)(2,1)}, u32[]{:S(2)}, u32[]{:S(2)}) async-start(bf16[2,4,256,1024]{2,3,0,1:T(8,128)(2,1)} %bitcast.216), calls=%async_computation.3 | async-start | bytes 8388608 | tf_op jit(solution)/shard_map/all_to_all | solution.py:139
  443.1 9.0 %copy-start.1 = (bf16[8,512,128]{2,1,0:T(8,128)(2,1)S(1)}, bf16[8,512,128]{2,1,0:T(8,128)(2,1)}, u32[]{:S(2)}) copy-start(bf16[8,512,128]{2,1,0:T(8,128)(2,1)} %param.5) | copy-start | bytes 3145732
where the time goes:
time: 459 us; the launch traced here: 452 us
  blocking collectives  148 us (32%)
  waiting for transfers between devices  105 us (23%)
  matrix products  85.8 us (19%)
  local copies, waits for them, and re-layouts  84.9 us (18%)
  starting transfers between devices  21.2 us (5%)
  other arithmetic  7.26 us (2%)
    all_to_all x1, blocking collectives, body(): lax.all_to_all(as_sent(columns_done), 'pulse', split_axis=2, concat_axis=...  95.8 us
    all_to_all x1, waiting for transfers between devices, body(): lax.all_to_all(shaped.astype(jnp.bfloat16), 'pulse', split_axis=1, concat...  93.5 us
    all_to_all x1, blocking collectives, body(): lax.all_to_all(lax.all_to_all(as_sent(columns_done), 'pulse', split_axis=...  51.9 us
    convert_element_type x1, local copies, waits for them, and re-layouts, as_sent(): a.astype(jnp.bfloat16)  25.5 us
    all_to_all x3, local copies, waits for them, and re-layouts, body(): lax.all_to_all(as_sent(columns_done), 'pulse', split_axis=2, concat_axis=...  20.1 us
    dot_general x3, matrix products, spectral(): jnp.einsum('...km,mj->...jk', turned_imag, sin_inner, precision=highest)  13.9 us
    dot_general x3, matrix products, spectral(): jnp.einsum('...km,mj->...jk', turned_real, sin_inner, precision=highest)  13.4 us
    dot_general x3, matrix products, spectral(): jnp.einsum('...km,mj->...jk', turned_imag, cos_inner, precision=highest)  13 us
  transfers between devices with their start and end apart: 6, of which 3 were waited for; matrix products, arithmetic and copies ran while one was open for 3% of the time, Pallas kernels for 0%

commit v1 on v0

--- a/solution.py
+++ b/solution.py
@@ -142,12 +142,22 @@
     real_out, imag_out = spectral(pieces[0], pieces[1], 1.0)
     columns_done = jnp.stack([real_out, imag_out])
     columns_done = columns_done.reshape(2, pieces_each, band_rows * n_pulse)
-    moved = lax.all_to_all(
-        lax.all_to_all(as_sent(columns_done), "pulse", split_axis=2, concat_axis=1, tiled=True),
-        ("range", "sub"),
-        split_axis=2,
-        concat_axis=1,
-        tiled=True,
+    moved = jnp.concatenate(
+        lax.all_to_all(
+            jnp.stack(
+                jnp.split(
+                    lax.all_to_all(
+                        as_sent(columns_done), "pulse", split_axis=2, concat_axis=1, tiled=True
+                    ),
+                    lax.axis_size(("range", "sub")),
+                    axis=2,
+                )
+            ),
+            ("range", "sub"),
+            0,
+            0,
+        ),
+        axis=1,
     ).astype(columns_done.dtype)
     flipped = jnp.swapaxes(moved, 1, 2)
     real_out, imag_out = spectral(flipped[0], flipped[1], 1.0)

time: 459 us -> 437 us (0.952)
  local copies, waits for them, and re-layouts: 84.9 us -> 64.5 us
    all_to_all x3 -> x2, local copies, waits for them, and re-layouts: 20.1 us -> 8.85 us  [body(): lax.all_to_all(as_sent(columns_done), 'pulse', split_axis=2, concat_axis=...]
    all_to_all x2 -> x0, local copies, waits for them, and re-layouts: 9.69 us -> none  [body(): lax.all_to_all(lax.all_to_all(as_sent(columns_done), 'pulse', split_axis=...]
where the time goes in v1:
time: 437 us; the launch traced here: 431 us
  blocking collectives  146 us (33%)
  waiting for transfers between devices  105 us (24%)
  matrix products  85.4 us (20%)
  local copies, waits for them, and re-layouts  64.5 us (15%)
  starting transfers between devices  21 us (5%)
  other arithmetic  7.83 us (2%)
    all_to_all x1, blocking collectives, body(): lax.all_to_all(as_sent(columns_done), 'pulse', split_axis=2, concat_axis=...  95.8 us
    all_to_all x1, waiting for transfers between devices, body(): lax.all_to_all(shaped.astype(jnp.bfloat16), 'pulse', split_axis=1, concat...  93.6 us
    all_to_all x1, blocking collectives, body(): lax.all_to_all(jnp.stack(jnp.split(lax.all_to_all(as_sent(columns_done),...  50.7 us
    convert_element_type x1, local copies, waits for them, and re-layouts, as_sent(): a.astype(jnp.bfloat16)  25.5 us
    dot_general x3, matrix products, spectral(): jnp.einsum('...km,mj->...jk', turned_real, sin_inner, precision=highest)  13.5 us
    dot_general x3, matrix products, spectral(): jnp.einsum('...km,mj->...jk', turned_imag, sin_inner, precision=highest)  13.5 us
    dot_general x3, matrix products, spectral(): jnp.einsum('...km,mj->...jk', turned_imag, cos_inner, precision=highest)  13 us
    dot_general x3, matrix products, spectral(): jnp.einsum('...km,mj->...jk', turned_real, cos_inner, precision=highest)  12.9 us
  transfers between devices with their start and end apart: 6, of which 3 were waited for; matrix products, arithmetic and copies ran while one was open for 3% of the time, Pallas kernels for 0%

profile of v1, /device:TPU:0, one launch (start us, length us, event | category | flops | bytes accessed | tf_op | source)
XLA Modules:
  0.0 431.1 jit_solution(9116974509237830483)
XLA Ops:
  0.0 1.3 copy.124
  1.3 0.9 copy.125
  2.2 4.2 all-to-all-start
  6.5 0.3 fusion.119
  6.7 0.3 sine_multiply_fusion
  7.0 0.7 fusion.182
  7.7 0.2 select_reduce_fusion
  8.1 0.9 convolution_convert_fusion.1
  9.0 3.3 all-to-all-done
  12.3 0.7 broadcast_in_dim.10
  13.0 5.1 %all-to-all-start.2 = ((bf16[8,2,2048]{2,1,0:T(2,128)(2,1)}), bf16[8,2,2048]{2,1,0:T(2,128)(2,1)S(1)}, u32[]{:S(2)}, u32[]{:S(2)}) async-start(bf16[8,2,2048]{2,1,0:T(2,128)(2,1)} %bitcast.30), calls=%async_computation.2 | async-start | bytes 131072 | tf_op jit(solution)/shard_map/all_to_all | solution.py:111
  18.5 0.5 fusion.67
  19.0 0.5 fusion.73
  19.7 0.5 fusion.44
  20.2 0.5 fusion.45
  20.7 0.7 fusion.57
  21.4 0.7 fusion.59
  22.1 0.7 fusion.48
  22.9 0.7 fusion.49
  23.7 0.5 convolution_convert_fusion
  24.2 1.0 copy.132
  25.2 6.2 %all-to-all-start.1 = ((bf16[8,2,2,4096]{3,2,1,0:T(2,128)(2,1)}), bf16[8,2,2,4096]{3,2,1,0:T(2,128)(2,1)S(1)}, u32[]{:S(2)}, u32[]{:S(2)}) async-start(bf16[8,2,2,4096]{3,2,1,0:T(2,128)(2,1)} %copy.132), calls=%async_computation.1 | async-start | bytes 524288 | tf_op jit(solution)/shard_map/all_to_all | solution.py:108
  31.6 8.1 %all-to-all-done.1 = bf16[8,2,2,4096]{3,2,1,0:T(2,128)(2,1)S(1)} async-done(((bf16[8,2,2,4096]{3,2,1,0:T(2,128)(2,1)}), bf16[8,2,2,4096]{3,2,1,0:T(2,128)(2,1)S(1)}, u32[]{:S(2)}, u32[]{:S(2)}) %all-to-all-start.1) | async-done | bytes 262176 | tf_op jit(solution)/shard_map/all_to_all | solution.py:108
  39.8 0.3 fusion.50
  40.3 1.3 convert_bitcast_fusion.1
  41.6 1.3 convert_bitcast_fusion
  42.9 2.2 add_convert_fusion
  45.1 2.3 copy.217
  47.4 5.3 %all-to-all-start.3 = ((bf16[2,4,256,1024]{2,3,0,1:T(8,128)(2,1)}), bf16[2,4,256,1024]{2,3,0,1:T(8,128)(2,1)}, u32[]{:S(2)}, u32[]{:S(2)}) async-start(bf16[2,4,256,1024]{2,3,0,1:T(8,128)(2,1)} %bitcast.222), calls=%async_computation.3 | async-start | bytes 8388608 | tf_op jit(solution)/shard_map/all_to_all | solution.py:139
  52.8 93.6 %all-to-all-done.3 = bf16[2,4,256,1024]{2,3,0,1:T(8,128)(2,1)} async-done(((bf16[2,4,256,1024]{2,3,0,1:T(8,128)(2,1)}), bf16[2,4,256,1024]{2,3,0,1:T(8,128)(2,1)}, u32[]{:S(2)}, u32[]{:S(2)}) %all-to-all-start.3) | async-done | bytes 4194336 | tf_op jit(solution)/shard_map/all_to_all | solution.py:139
  146.4 2.5 copy.218
  148.9 0.3 fusion.261
  149.2 2.8 fusion.38
  152.0 2.8 fusion.40
  154.8 2.9 convolution_add_fusion.1
  157.7 4.7 %fusion.1 = (f32[256,64,64]{0,1,2:T(8,128)S(1)}, f32[256,64,64]{0,1,2:T(8,128)S(1)}) fusion(f32[64,256,64]{1,0,2:T(8,128)S(1)} %convolution_add_fusion.1, f32[64,64]{0,1:T(8,128)S(1)} %get-tuple-element.21, f32[64,64]{0,1:T(8,128)S(1)} %get-tuple-element.22, f32[64,256,64]{1,0,2:T(8,128)S(1)} %fusion.40, bf16[256,64,64]{0,2,1:T(8,128)(2,1)S(1)} %bitcast.216), kind=kOutput, calls=%fused_computation.9 | convolution fusion | flops 812703744 | bytes 18907136 | tf_op jit(solution)/shard_map/...nm,nk->...km/dot_general | solution.py:42
  162.4 6.3 %fusion.12 = f32[64,256,64]{1,0,2:T(8,128)S(1)} fusion(f32[256,64,64]{0,1,2:T(8,128)S(1)} %get-tuple-element.8), kind=kOutput, calls=%fused_computation.31 | convolution fusion | flops 805363712 | bytes 8388608 | tf_op jit(solution)/shard_map/...km,mj->...jk/dot_general | solution.py:59
  168.7 6.3 %fusion.14 = f32[64,256,64]{1,0,2:T(8,128)S(1)} fusion(f32[256,64,64]{0,1,2:T(8,128)S(1)} %get-tuple-element.8), kind=kOutput, calls=%fused_computation.33 | convolution fusion | flops 805363712 | bytes 8388608 | tf_op jit(solution)/shard_map/...km,mj->...jk/dot_general | solution.py:56
  175.0 6.0 %fusion.25 = bf16[1,256,64,64]{1,2,3,0:T(8,128)(2,1)S(1)} fusion(f32[64,256,64]{1,0,2:T(8,128)S(1)} %fusion.12, f32[256,64,64]{0,1,2:T(8,128)S(1)} %get-tuple-element.7), kind=kOutput, calls=%fused_computation.45 | convolution fusion | flops 808509440 | bytes 10485760 | tf_op jit(solution)/shard_map/...km,mj->...jk/dot_general | solution.py:57
  181.0 1.2 copy.147
  182.2 5.9 %fusion.24 = bf16[1,256,64,64]{1,2,3,0:T(8,128)(2,1)S(1)} fusion(f32[64,256,64]{1,0,2:T(8,128)S(1)} %fusion.14, f32[256,64,64]{0,1,2:T(8,128)S(1)} %get-tuple-element.7), kind=kOutput, calls=%fused_computation.44 | convolution fusion | flops 808509440 | bytes 10485760 | tf_op jit(solution)/shard_map/...km,mj->...jk/dot_general | solution.py:54
  188.1 1.2 copy.144
  189.3 0.4 maximum_bitcast_fusion
  189.7 25.5 %copy.148 = bf16[2,256,4096]{1,0,2:T(2,128)(2,1)S(1)} copy(bf16[2,256,4096]{1,2,0:T(8,128)(2,1)S(1)} %maximum_bitcast_fusion) | data formatting | bytes 8388608 | tf_op jit(solution)/shard_map/convert_element_type | solution.py:21
  215.1 95.8 %all_to_all.63 = bf16[2,256,4096]{1,0,2:T(2,128)(2,1)S(1)} all-to-all(bf16[2,256,4096]{1,0,2:T(2,128)(2,1)S(1)} %copy.148), channel_id=1, replica_groups=mesh['groups'=2,'pulse'=4,'range'=2,'sub'=2] {'pulse'}, dimensions={2} | all-to-all | bytes 8388608 | tf_op jit(solution)/shard_map/all_to_all | solution.py:149
  310.9 2.6 copy.149
  313.5 6.3 %copy.150 = bf16[2,4,256,1024]{3,2,1,0:T(8,128)(2,1)} copy(bf16[2,4,256,1024]{2,3,1,0:T(8,128)(2,1)} %bitcast.226) | data formatting | bytes 8388608 | tf_op jit(solution)/shard_map/all_to_all | solution.py:149
  319.7 2.5 slice_bitcast_fusion.3
  322.2 0.6 pad_maximum_fusion.1
  322.8 50.7 %all_to_all.64 = bf16[4,2,1024,256]{3,2,1,0:T(8,128)(2,1)S(1)} all-to-all(bf16[4,2,1024,256]{3,2,1,0:T(8,128)(2,1)S(1)} %pad_maximum_fusion.1), channel_id=1, replica_groups=mesh['groups'=2,'pulse'=4,'range'=2,'sub'=2] {'range','sub'}, dimensions={0} | all-to-all | bytes 8388608 | tf_op jit(solution)/shard_map/all_to_all | solution.py:146
  373.5 0.3 copy.151
  373.8 0.3 fusion.260
  374.1 2.8 fusion.32
  376.9 2.8 fusion.34
  379.7 2.9 convolution_add_fusion
  382.6 4.7 %subtract_bitcast_fusion = (f32[256,64,64]{0,1,2:T(8,128)S(1)}, f32[256,64,64]{0,1,2:T(8,128)S(1)}) fusion(f32[64,256,64]{1,0,2:T(8,128)S(1)} %convolution_add_fusion, f32[64,64]{0,1:T(8,128)S(1)} %get-tuple-element.21, f32[64,64]{0,1:T(8,128)S(1)} %get-tuple-element.22, f32[64,256,64]{1,0,2:T(8,128)S(1)} %fusion.34, bf16[256,64,64]{0,2,1:T(8,128)(2,1)S(1)} %bitcast.214), kind=kOutput, calls=%fused_computation.18 | convolution fusion | flops 812703744 | bytes 18907136 | tf_op jit(solution)/shard_map/...nm,nk->...km/dot_general | solution.py:42
  387.3 6.0 %fusion.4 = f32[64,256,64]{1,0,2:T(8,128)S(1)} fusion(f32[256,64,64]{0,1,2:T(8,128)S(1)} %get-tuple-element.6), kind=kOutput, calls=%fused_computation.23 | convolution fusion | flops 805363712 | bytes 8388608 | tf_op jit(solution)/shard_map/...km,mj->...jk/dot_general | solution.py:59
  393.3 6.5 %fusion.6 = f32[64,256,64]{1,0,2:T(8,128)S(1)} fusion(f32[256,64,64]{0,1,2:T(8,128)S(1)} %get-tuple-element.6), kind=kOutput, calls=%fused_computation.25 | convolution fusion | flops 805363712 | bytes 8388608 | tf_op jit(solution)/shard_map/...km,mj->...jk/dot_general | solution.py:56
  399.8 6.4 %multiply_bitcast_fusion.1 = f32[256,64,64]{0,1,2:T(8,128)S(1)} fusion(f32[64,256,64]{1,0,2:T(8,128)S(1)} %fusion.6, f32[256,64,64]{0,1,2:T(8,128)S(1)} %get-tuple-element.5), kind=kOutput, calls=%fused_computation.16 | convolution fusion | flops 807460864 | bytes 12582912 | tf_op jit(solution)/shard_map/...km,mj->...jk/dot_general | solution.py:54
  406.2 6.8 %multiply_bitcast_fusion = f32[256,64,64]{0,1,2:T(8,128)S(1)} fusion(f32[64,256,64]{1,0,2:T(8,128)S(1)} %fusion.4, f32[256,64,64]{0,1,2:T(8,128)S(1)} %get-tuple-element.5), kind=kOutput, calls=%fused_computation.15 | convolution fusion | flops 807460864 | bytes 12582912 | tf_op jit(solution)/shard_map/...km,mj->...jk/dot_general | solution.py:57
  413.0 2.4 copy.161
  415.5 2.4 copy.158
  417.9 3.8 pad_maximum_fusion
  421.7 9.0 %copy.162 = f32[2,256,4096]{2,1,0:T(8,128)} copy(f32[2,256,4096]{1,2,0:T(8,128)} %pad_maximum_fusion) | data formatting | bytes 16777216 | tf_op jit(solution)/shard_map/stack | solution.py:164
  (26 shorter events, 1.6 us)
Async XLA Ops:
  0.0 39.8 %copy-start = (bf16[8,512,128]{2,1,0:T(8,128)(2,1)S(1)}, bf16[8,512,128]{2,1,0:T(8,128)(2,1)}, u32[]{:S(2)}) copy-start(bf16[8,512,128]{2,1,0:T(8,128)(2,1)} %param.5) | copy-start | bytes 3145732
  2.2 10.1 %all-to-all-start = ((bf16[2,2,4,8192]{3,2,0,1:T(4,128)(2,1)}), bf16[2,2,4,8192]{3,2,0,1:T(4,128)(2,1)S(1)}, u32[]{:S(2)}, u32[]{:S(2)}) async-start(bf16[2,2,4,8192]{3,2,0,1:T(4,128)(2,1)} %copy.125), calls=%async_computation | async-start | bytes 524288 | tf_op jit(solution)/shard_map/all_to_all | solution.py:76
  13.0 12.2 %all-to-all-start.2 = ((bf16[8,2,2048]{2,1,0:T(2,128)(2,1)}), bf16[8,2,2048]{2,1,0:T(2,128)(2,1)S(1)}, u32[]{:S(2)}, u32[]{:S(2)}) async-start(bf16[8,2,2048]{2,1,0:T(2,128)(2,1)} %bitcast.30), calls=%async_computation.2 | async-start | bytes 131072 | tf_op jit(solution)/shard_map/all_to_all | solution.py:111
  25.2 14.4 %all-to-all-start.1 = ((bf16[8,2,2,4096]{3,2,1,0:T(2,128)(2,1)}), bf16[8,2,2,4096]{3,2,1,0:T(2,128)(2,1)S(1)}, u32[]{:S(2)}, u32[]{:S(2)}) async-start(bf16[8,2,2,4096]{3,2,1,0:T(2,128)(2,1)} %copy.132), calls=%async_computation.1 | async-start | bytes 524288 | tf_op jit(solution)/shard_map/all_to_all | solution.py:108
  31.5 10.1 %collective-permute-start.1 = (bf16[16,2048]{1,0:T(8,128)(2,1)S(1)}, bf16[16,2048]{1,0:T(8,128)(2,1)S(1)}, u32[]{:S(2)}, u32[]{:S(2)}) collective-permute-start(bf16[16,2048]{1,0:T(8,128)(2,1)S(1)} %reshape.312), channel_id=1, source_target_pairs={{0,1},{1,0},{2,3},{3,2},{4,5},{5,4},{6,7},{7,6},{8,9},{9,8},{10,11... | collective-permute-start | bytes 196616 | tf_op jit(solution)/shard_map/ppermute | solution.py:17
  40.2 1.4 collective-permute-start
  47.4 99.0 %all-to-all-start.3 = ((bf16[2,4,256,1024]{2,3,0,1:T(8,128)(2,1)}), bf16[2,4,256,1024]{2,3,0,1:T(8,128)(2,1)}, u32[]{:S(2)}, u32[]{:S(2)}) async-start(bf16[2,4,256,1024]{2,3,0,1:T(8,128)(2,1)} %bitcast.222), calls=%async_computation.3 | async-start | bytes 8388608 | tf_op jit(solution)/shard_map/all_to_all | solution.py:139
  421.7 9.0 %copy-start.1 = (bf16[8,512,128]{2,1,0:T(8,128)(2,1)S(1)}, bf16[8,512,128]{2,1,0:T(8,128)(2,1)}, u32[]{:S(2)}) copy-start(bf16[8,512,128]{2,1,0:T(8,128)(2,1)} %param.5) | copy-start | bytes 3145732
